TPU v7x, 256 devices: a whole 4x4x8 slice. The times are simulated.
256 devices in a mesh: row: 8 (over x, z_hi), col: 32 (over y, z_lo, core).
Axes of the slice: x: 4, y: 4, z: 8 (z_hi: 2, z_lo: 4; z = z_hi * 4 + z_lo), core: 2. Of those that a mesh axis runs over, the one named last changes fastest.
Arguments:
- matrix: float32 [16384, 16384], P('row', 'col'), may hold values from -6 to 6, as said below
- vectors: float32 [2, 16384, 128], P(None, ('row', 'col')), may hold values from -0.16 to 0.16
- tfactor: float32 [2, 128, 128], replicated, may hold values from -0.5 to 0.5
Outputs:
- updated: float32 [16384, 16384], P('row', 'col')
Inputs may be any that keep to these rules, and one draw needn't show every extreme that they name: matrix is symmetric: matrix[i, j] equals matrix[j, i].
All inputs are finite; a program needn't handle non-finite values.
Results may differ from a plain program's by a relative error of at most 0.00012.
Values sent between devices are 32-bit elements; how exact they have to be, the bound alone decides.
A program may use at most 64 MiB of HBM per device.

v0:
```python
import jax
import jax.numpy as jnp
from jax import lax
from jax.sharding import PartitionSpec as P

highest = lax.Precision.HIGHEST


def spread(block, axis, source):
    block = jnp.where(lax.axis_index(axis) == source, block, jnp.zeros_like(block))
    return lax.psum(block, axis)


def mat_product(left, right):
    return jnp.dot(left, right, precision=highest, preferred_element_type=jnp.float32)


def body(matrix, vectors, tfactor):
    rows_here, cols_here = matrix.shape
    panels = vectors.shape[0]
    own_count = vectors.shape[1]
    row_total = lax.axis_size("row")
    col_total = lax.axis_size("col")
    row_index = lax.axis_index("row")
    col_index = lax.axis_index("col")
    owner_row = col_index * row_total // col_total
    offset = col_index * cols_here - owner_row * rows_here
    v_rows = lax.all_gather(vectors, "col", axis=1, tiled=True)
    v_local = lax.dynamic_slice_in_dim(v_rows, offset, cols_here, 1)
    v_cols = spread(v_local, "row", owner_row)
    current = matrix
    for panel_index in range(panels):
        vector_i = v_rows[panel_index]
        vector_j = v_cols[panel_index]
        own_rows = vectors[panel_index]
        factor = jnp.triu(tfactor[panel_index])

        def partial_rows(begin_row, span_rows, current=current, vector_j=vector_j):
            return mat_product(current, vector_j)

        summed = lax.psum_scatter(
            partial_rows(jnp.int32(0), own_count * lax.axis_size("col")),
            "col",
            scatter_dimension=0,
            tiled=True,
        )
        ymatrix = mat_product(summed, factor)
        gram_matrix = lax.psum(mat_product(own_rows.T, ymatrix), ("row", "col"))
        w_own = ymatrix - 0.5 * mat_product(own_rows, mat_product(factor.T, gram_matrix))
        w_all = lax.all_gather(w_own, ("row", "col"), axis=0, tiled=True)
        w_i = lax.dynamic_slice_in_dim(w_all, row_index * rows_here, rows_here, 0)
        w_j = lax.dynamic_slice_in_dim(w_all, col_index * cols_here, cols_here, 0)
        current = current - mat_product(vector_i, w_j.T) - mat_product(w_i, vector_j.T)
    return current


def solution(mesh):
    return jax.shard_map(
        body,
        mesh=mesh,
        in_specs=(P("row", "col"), P(None, ("row", "col"), None), P()),
        out_specs=P("row", "col"),
        check_vma=False,
    )
```

profile of v0, /device:TPU:32, one launch (start us, length us, event | category | flops | bytes accessed | tf_op | source)
XLA Modules:
  0.0 1845.8 jit_solution(2119604143348090658)
XLA Ops:
  7.3 64.0 %all-gather.4.cloned.1.call-done = f32[2,2048,128]{2,1,0:T(8,128)} async-done(((f32[2,64,128]{2,1,0:T(8,128)}), f32[2,2048,128]{2,1,0:T(8,128)}) %all-gather.4.cloned.1.call-update) | async-done | bytes 2097168 | tf_op jit(solution)/shard_map/all_gather | solution.py:28
  71.3 1.9 dynamic-slice_select_fusion
  73.2 110.7 %all-reduce.4.cloned.1.call-done = f32[2,512,128]{2,1,0:T(8,128)} async-done(((f32[2,512,128]{2,1,0:T(8,128)}), f32[2,512,128]{2,1,0:T(8,128)}) %all-reduce.4.cloned.1.call-update) | async-done | bytes 524304 | tf_op jit(solution)/shard_map/psum | solution.py:11
  184.0 6.7 convolution_bitcast_fusion
  190.7 1.3 copy.14
  192.1 136.8 %reduce-scatter.7.cloned.1.call-done = f32[64,128]{1,0:T(8,128)} async-done(((f32[2048,128]{1,0:T(8,128)}), f32[64,128]{1,0:T(8,128)}) %reduce-scatter.7.cloned.1.call-update) | async-done | bytes 32784
  328.9 1.0 fusion.14
  330.0 0.9 convolution_bitcast_fusion.2
  331.0 245.8 %all-reduce.6.cloned.1.call-done = f32[128,128]{0,1:T(8,128)} async-done(((f32[128,128]{0,1:T(8,128)}), f32[128,128]{0,1:T(8,128)}) %all-reduce.6.cloned.1.call-update) | async-done | bytes 65552 | tf_op jit(solution)/shard_map/psum | solution.py:48
  576.7 1.2 fusion.13
  578.8 5.5 copy.8
  584.3 412.1 %all-gather.6.cloned.1.call-done = f32[16384,128]{1,0:T(8,128)} async-done(((f32[64,128]{1,0:T(8,128)}), f32[16384,128]{1,0:T(8,128)}) %all-gather.6.cloned.1.call-update) | async-done | bytes 8388624 | tf_op jit(solution)/shard_map/all_gather | solution.py:50
  996.5 4.9 fusion.8
  1001.4 4.9 fusion.1
  1006.3 2.0 copy-done
  1008.3 8.1 fusion.12
  1016.5 138.2 %reduce-scatter.5.cloned.1.call-done = f32[64,128]{1,0:T(8,128)} async-done(((f32[2048,128]{1,0:T(8,128)}), f32[64,128]{1,0:T(8,128)}) %reduce-scatter.5.cloned.1.call-update) | async-done | bytes 32784 | tf_op jit(solution)/shard_map/reduce_scatter | solution.py:41
  1154.7 1.0 fusion.16
  1156.7 245.8 %all-reduce.8.cloned.1.call-done = f32[128,128]{0,1:T(8,128)} async-done(((f32[128,128]{0,1:T(8,128)}), f32[128,128]{0,1:T(8,128)}) %all-reduce.8.cloned.1.call-update) | async-done | bytes 65552 | tf_op jit(solution)/shard_map/psum | solution.py:48
  1402.5 1.2 fusion.15
  1404.5 417.7 %all-gather.8.cloned.1.call-done = f32[16384,128]{1,0:T(8,128)} async-done(((f32[64,128]{1,0:T(8,128)}), f32[16384,128]{1,0:T(8,128)}) %all-gather.8.cloned.1.call-update) | async-done | bytes 8388624 | tf_op jit(solution)/shard_map/all_gather | solution.py:50
  1822.2 4.9 fusion.6
  1827.1 6.5 fusion
  1833.6 5.3 copy.11
  (33 shorter events, 3.7 us)
Async XLA Ops:
  6.5 64.7 %all-gather.4.cloned.1.call-start = ((), (), s32[]{:S(2)}) async-start(), calls=%async_computation.2 | async-start | bytes 2162688 | tf_op jit(solution)/shard_map/all_gather | solution.py:28
  7.3 176.7 %all-reduce.4.cloned.1.call-start = ((), (), s32[]{:S(2)}) async-start(), calls=%async_computation.3 | async-start | bytes 1048576 | tf_op jit(solution)/shard_map/psum | solution.py:11
  73.2 255.8 %copy-start.6 = (f32[2,128,128]{2,1,0:T(8,128)S(1)}, f32[2,128,128]{2,1,0:T(8,128)}, u32[]{:S(2)}) copy-start(f32[2,128,128]{2,1,0:T(8,128)} %param.5) | copy-start | bytes 393220
  73.2 256.8 %copy-start.5 = (f32[2,64,128]{2,1,0:T(8,128)S(1)}, f32[2,64,128]{2,1,0:T(8,128)}, u32[]{:S(2)}) copy-start(f32[2,64,128]{2,1,0:T(8,128)} %param.4) | copy-start | bytes 196612
  73.2 255.7 %reduce-scatter.7.cloned.1.call-start = ((), (), s32[]{:S(2)}) async-start(), calls=%async_computation.9 | async-start | bytes 1081344
  192.1 384.7 %all-reduce.6.cloned.1.call-start = ((), (), s32[]{:S(2)}) async-start(), calls=%async_computation.4 | async-start | bytes 131072 | tf_op jit(solution)/shard_map/psum | solution.py:48
  330.9 665.6 %all-gather.6.cloned.1.call-start = ((), (), s32[]{:S(2)}) async-start(), calls=%async_computation.5 | async-start | bytes 8421376 | tf_op jit(solution)/shard_map/all_gather | solution.py:50
  578.8 576.0 %reduce-scatter.5.cloned.1.call-start = ((), (), s32[]{:S(2)}) async-start(), calls=%async_computation.6 | async-start | bytes 1081344 | tf_op jit(solution)/shard_map/reduce_scatter | solution.py:41
  578.8 417.6 %copy-start.4 = (f32[2,512,128]{2,1,0:T(8,128)S(1)}, f32[2,512,128]{2,1,0:T(8,128)}, u32[]{:S(2)}) copy-start(f32[2,512,128]{2,1,0:T(8,128)} %all-reduce.4.cloned.1.call-done) | copy-start | bytes 1572868
  578.8 422.5 %copy-start.3 = (f32[2,2048,128]{2,1,0:T(8,128)S(1)}, f32[2,2048,128]{2,1,0:T(8,128)}, u32[]{:S(2)}) copy-start(f32[2,2048,128]{2,1,0:T(8,128)} %all-gather.4.cloned.1.call-done) | copy-start | bytes 6291460
  996.5 4.9 copy-start.2
  1006.3 2.0 copy-start
  1016.4 386.1 %all-reduce.8.cloned.1.call-start = ((), (), s32[]{:S(2)}) async-start(), calls=%async_computation.7 | async-start | bytes 131072 | tf_op jit(solution)/shard_map/psum | solution.py:48
  1156.7 665.5 %all-gather.8.cloned.1.call-start = ((), (), s32[]{:S(2)}) async-start(), calls=%async_computation.8 | async-start | bytes 8421376 | tf_op jit(solution)/shard_map/all_gather | solution.py:50
  1822.2 4.9 copy-start.1
Sparse Core Ops, SparseCore 0:
  9.2 62.0 all-gather.3
  73.9 110.0 all-reduce.3
  192.2 136.7 reduce-scatter.6
  334.3 242.4 all-reduce.5
  578.9 417.5 all-gather.5
  1016.6 138.1 reduce-scatter.4
  1160.2 242.2 all-reduce.7
  1404.7 417.5 all-gather.7
where the time goes:
time: 1850 us
  waiting for transfers between devices  1770 us (96%)
  matrix products  43.8 us (2%)
    all_gather x2, waiting for transfers between devices, body(): w_all = lax.all_gather(w_own, ('row', 'col'), axis=0, tiled=True)  830 us
    psum x2, waiting for transfers between devices, body(): gram_matrix = lax.psum(mat_product(own_rows.T, ymatrix), ('row', 'col'))  492 us
    reduce_scatter x1, waiting for transfers between devices, body(): lax.psum_scatter(partial_rows(jnp.int32(0), own_count * lax.axis_size('co...  138 us
    unnamed x9, waiting for transfers between devices  138 us
    psum x1, waiting for transfers between devices, spread(): return lax.psum(block, axis)  111 us
    all_gather x1, waiting for transfers between devices, body(): v_rows = lax.all_gather(vectors, 'col', axis=1, tiled=True)  64 us
    dot_general x14, matrix products, mat_product(): jnp.dot(left, right, precision=highest, preferred_element_type=jnp.float32)  43.8 us
  transfers between devices with their start and end apart: 8, of which 8 were waited for; matrix products, arithmetic and copies ran while one was open for 0% of the time, Pallas kernels for 0%

commit v1 on v0

--- a/solution.py
+++ b/solution.py
@@ -4,6 +4,12 @@
 from jax.sharding import PartitionSpec as P
 
 highest = lax.Precision.HIGHEST
+
+
+def summed_here(x, name):
+    parts = lax.all_gather(x, name, axis=0, tiled=False)
+    acc = parts.sum(axis=0)
+    return acc
 
 
 def spread(block, axis, source):
@@ -45,7 +51,7 @@
             tiled=True,
         )
         ymatrix = mat_product(summed, factor)
-        gram_matrix = lax.psum(mat_product(own_rows.T, ymatrix), ("row", "col"))
+        gram_matrix = summed_here(mat_product(own_rows.T, ymatrix), ("row", "col"))
         w_own = ymatrix - 0.5 * mat_product(own_rows, mat_product(factor.T, gram_matrix))
         w_all = lax.all_gather(w_own, ("row", "col"), axis=0, tiled=True)
         w_i = lax.dynamic_slice_in_dim(w_all, row_index * rows_here, rows_here, 0)

time: 1850 us -> 2270 us (1.23)
  waiting for transfers between devices: 1770 us -> 2150 us
  local copies, waits for them, and re-layouts: 14.2 us -> 42.4 us
    all_gather x0 -> x2, waiting for transfers between devices: none -> 867 us  [summed_here(): parts = lax.all_gather(x, name, axis=0, tiled=False)]
    psum x2 -> x0, waiting for transfers between devices: 492 us -> none  [body(): gram_matrix = lax.psum(mat_product(own_rows.T, ymatrix), ('row', 'col'))]
    unnamed x16 -> x18, local copies, waits for them, and re-layouts: 8.84 us -> 37 us
where the time goes in v1:
time: 2270 us
  waiting for transfers between devices  2150 us (95%)
  local copies, waits for them, and re-layouts  42.4 us (2%)
  matrix products  42.2 us (2%)
    all_gather x2, waiting for transfers between devices, summed_here(): parts = lax.all_gather(x, name, axis=0, tiled=False)  867 us
    all_gather x2, waiting for transfers between devices, body(): w_all = lax.all_gather(w_own, ('row', 'col'), axis=0, tiled=True)  832 us
    reduce_scatter x1, waiting for transfers between devices, body(): lax.psum_scatter(partial_rows(jnp.int32(0), own_count * lax.axis_size('co...  138 us
    unnamed x9, waiting for transfers between devices  138 us
    psum x1, waiting for transfers between devices, spread(): return lax.psum(block, axis)  111 us
    all_gather x1, waiting for transfers between devices, body(): v_rows = lax.all_gather(vectors, 'col', axis=1, tiled=True)  64 us
  transfers between devices with their start and end apart: 8, of which 8 were waited for; matrix products, arithmetic and copies ran while one was open for 0% of the time, Pallas kernels for 0%

profile of v1, /device:TPU:32, one launch (start us, length us, event | category | flops | bytes accessed | tf_op | source)
XLA Modules:
  0.0 2266.3 jit_solution(6753853804692090868)
XLA Ops:
  7.3 64.0 %all-gather.8.cloned.1.call-done = f32[2,2048,128]{2,1,0:T(8,128)} async-done(((f32[2,64,128]{2,1,0:T(8,128)}), f32[2,2048,128]{2,1,0:T(8,128)}) %all-gather.8.cloned.1.call-update) | async-done | bytes 2097168 | tf_op jit(solution)/shard_map/all_gather | solution.py:34
  71.3 1.9 dynamic-slice_select_fusion
  73.2 110.7 %all-reduce.2.cloned.1.call-done = f32[2,512,128]{2,1,0:T(8,128)} async-done(((f32[2,512,128]{2,1,0:T(8,128)}), f32[2,512,128]{2,1,0:T(8,128)}) %all-reduce.2.cloned.1.call-update) | async-done | bytes 524304 | tf_op jit(solution)/shard_map/psum | solution.py:17
  184.0 6.7 convolution_bitcast_fusion
  190.7 1.3 copy.14
  192.1 136.8 %reduce-scatter.7.cloned.1.call-done = f32[64,128]{1,0:T(8,128)} async-done(((f32[2048,128]{1,0:T(8,128)}), f32[64,128]{1,0:T(8,128)}) %reduce-scatter.7.cloned.1.call-update) | async-done | bytes 32784
  328.9 1.0 fusion.14
  331.0 433.8 %all-gather.14.cloned.1.call-done = f32[32768,128]{0,1:T(8,128)} async-done(((f32[128,128]{0,1:T(8,128)}), f32[32768,128]{0,1:T(8,128)}) %all-gather.14.cloned.1.call-update) | async-done | bytes 16777232 | tf_op jit(solution)/shard_map/all_gather | solution.py:10
  764.8 14.1 copy.16
  778.9 8.0 bitcast_reduce_fusion.1
  788.2 5.5 copy.8
  793.7 413.1 %all-gather.10.cloned.1.call-done = f32[16384,128]{1,0:T(8,128)} async-done(((f32[64,128]{1,0:T(8,128)}), f32[16384,128]{1,0:T(8,128)}) %all-gather.10.cloned.1.call-update) | async-done | bytes 8388624 | tf_op jit(solution)/shard_map/all_gather | solution.py:56
  1206.8 4.9 fusion.8
  1211.7 4.9 fusion.1
  1216.6 2.0 copy-done
  1218.6 8.1 fusion.12
  1226.8 138.3 %reduce-scatter.5.cloned.1.call-done = f32[64,128]{1,0:T(8,128)} async-done(((f32[2048,128]{1,0:T(8,128)}), f32[64,128]{1,0:T(8,128)}) %reduce-scatter.5.cloned.1.call-update) | async-done | bytes 32784 | tf_op jit(solution)/shard_map/reduce_scatter | solution.py:47
  1367.1 433.6 %all-gather.16.cloned.1.call-done = f32[32768,128]{0,1:T(8,128)} async-done(((f32[128,128]{0,1:T(8,128)}), f32[32768,128]{0,1:T(8,128)}) %all-gather.16.cloned.1.call-update) | async-done | bytes 16777232 | tf_op jit(solution)/shard_map/all_gather | solution.py:10
  1800.7 14.1 copy.17
  1814.8 8.0 bitcast_reduce_fusion
  1824.1 418.6 %all-gather.12.cloned.1.call-done = f32[16384,128]{1,0:T(8,128)} async-done(((f32[64,128]{1,0:T(8,128)}), f32[16384,128]{1,0:T(8,128)}) %all-gather.12.cloned.1.call-update) | async-done | bytes 8388624 | tf_op jit(solution)/shard_map/all_gather | solution.py:56
  2242.7 4.9 fusion.6
  2247.6 6.5 fusion
  2254.1 5.3 copy.11
  (37 shorter events, 6.3 us)
Async XLA Ops:
  6.5 64.7 %all-gather.8.cloned.1.call-start = ((), (), s32[]{:S(2)}) async-start(), calls=%async_computation.2 | async-start | bytes 2162688 | tf_op jit(solution)/shard_map/all_gather | solution.py:34
  7.3 176.7 %all-reduce.2.cloned.1.call-start = ((), (), s32[]{:S(2)}) async-start(), calls=%async_computation.3 | async-start | bytes 1048576 | tf_op jit(solution)/shard_map/psum | solution.py:17
  73.2 255.8 %copy-start.6 = (f32[2,128,128]{2,1,0:T(8,128)S(1)}, f32[2,128,128]{2,1,0:T(8,128)}, u32[]{:S(2)}) copy-start(f32[2,128,128]{2,1,0:T(8,128)} %param.5) | copy-start | bytes 393220
  73.2 256.8 %copy-start.5 = (f32[2,64,128]{2,1,0:T(8,128)S(1)}, f32[2,64,128]{2,1,0:T(8,128)}, u32[]{:S(2)}) copy-start(f32[2,64,128]{2,1,0:T(8,128)} %param.4) | copy-start | bytes 196612
  73.2 255.7 %reduce-scatter.7.cloned.1.call-start = ((), (), s32[]{:S(2)}) async-start(), calls=%async_computation.9 | async-start | bytes 1081344
  192.1 572.7 %all-gather.14.cloned.1.call-start = ((), (), s32[]{:S(2)}) async-start(), calls=%async_computation.7 | async-start | bytes 16842752 | tf_op jit(solution)/shard_map/all_gather | solution.py:10
  330.9 875.8 %all-gather.10.cloned.1.call-start = ((), (), s32[]{:S(2)}) async-start(), calls=%async_computation.4 | async-start | bytes 8421376 | tf_op jit(solution)/shard_map/all_gather | solution.py:56
  788.1 577.0 %reduce-scatter.5.cloned.1.call-start = ((), (), s32[]{:S(2)}) async-start(), calls=%async_computation.5 | async-start | bytes 1081344 | tf_op jit(solution)/shard_map/reduce_scatter | solution.py:47
  788.2 418.6 %copy-start.4 = (f32[2,512,128]{2,1,0:T(8,128)S(1)}, f32[2,512,128]{2,1,0:T(8,128)}, u32[]{:S(2)}) copy-start(f32[2,512,128]{2,1,0:T(8,128)} %all-reduce.2.cloned.1.call-done) | copy-start | bytes 1572868
  788.2 423.5 %copy-start.3 = (f32[2,2048,128]{2,1,0:T(8,128)S(1)}, f32[2,2048,128]{2,1,0:T(8,128)}, u32[]{:S(2)}) copy-start(f32[2,2048,128]{2,1,0:T(8,128)} %all-gather.8.cloned.1.call-done) | copy-start | bytes 6291460
  1206.8 4.9 copy-start.2
  1216.6 2.0 copy-start
  1226.7 574.0 %all-gather.16.cloned.1.call-start = ((), (), s32[]{:S(2)}) async-start(), calls=%async_computation.8 | async-start | bytes 16842752 | tf_op jit(solution)/shard_map/all_gather | solution.py:10
  1367.1 875.6 %all-gather.12.cloned.1.call-start = ((), (), s32[]{:S(2)}) async-start(), calls=%async_computation.6 | async-start | bytes 8421376 | tf_op jit(solution)/shard_map/all_gather | solution.py:56
  2242.7 4.9 copy-start.1
Sparse Core Ops, SparseCore 0:
  9.2 62.0 all-gather.7
  73.9 110.0 all-reduce.1
  192.2 136.7 reduce-scatter.6
  331.0 433.7 all-gather.13
  788.2 418.4 all-gather.9
  1226.9 138.2 reduce-scatter.4
  1367.2 433.4 all-gather.15
  1824.2 418.4 all-gather.11
